TPU v7x, 512 devices: a whole 4x8x8 slice. The times are simulated.
512 devices in a mesh: ka: 128 (over y, x_hi, z), ta: 4 (over x_lo, core).
Axes of the slice: x: 4 (x_hi: 2, x_lo: 2; x = x_hi * 2 + x_lo), y: 8, z: 8, core: 2. Of those that a mesh axis runs over, the one named last changes fastest.
Arguments:
- green_hist: bfloat16 [256, 2, 2, 2, 512, 512], P('ka', None, None, None, 'ta'), may hold values from -6 to 6
- sigma_hist: bfloat16 [2, 2, 2, 512, 512], P(None, None, None, 'ta'), may hold values from -6 to 6
- prev_row: float32 [256, 2, 2, 2, 512], P('ka', None, None, None, 'ta'), may hold values from -8 to 8
- propagator: float32 [256, 2, 2, 2], P('ka'), may hold values from -3 to 3
- impurity_column: float32 [2, 2, 2, 512], P(None, None, None, 'ta'), may hold values from -3 to 3
- sigma_start: float32 [2, 2, 2, 512], P(None, None, None, 'ta'), may hold values from -6 to 6
Outputs:
- green_row: float32 [256, 2, 2, 2, 512], P('ka', None, None, None, 'ta')
- self_energy: float32 [2, 2, 2, 512], P(None, None, None, 'ta')
All inputs are finite; a program needn't handle non-finite values.
Results may differ from a plain program's by a relative error of at most 0.0031.
Values sent between devices are 32-bit elements; how exact they have to be, the bound alone decides.
No kernel may reach another device: no remote copies, remote signals or barrier semaphores. Data moves between devices by JAX's collectives and lax.ppermute only.
A program may use at most 64 MiB of HBM per device.

v0:
```python
import jax
import jax.numpy as jnp
from jax import lax
from jax.sharding import PartitionSpec as P

ITERS = 2


TIME_STEP = 0.02
COUPLING = 1.0


def sigma_block(self_energy):
    real_part = self_energy[0]
    imag_part = self_energy[1]
    upper = jnp.stack([real_part, -imag_part], axis=1)
    lower = jnp.stack([imag_part, real_part], axis=1)
    return jnp.stack([upper, lower], axis=0)


def row_block(green_row):
    real_part = green_row[:, 0]
    imag_part = green_row[:, 1]
    upper = jnp.stack([real_part, -imag_part], axis=2)
    lower = jnp.stack([imag_part, real_part], axis=2)
    return jnp.stack([upper, lower], axis=1)


def orbital_product(left, right):
    return jnp.sum(left[:, :, :, None, None] * right[:, None, :, :, :], axis=2)


def propagate(propagator, inner):
    prop_real = propagator[:, 0]
    prop_imag = propagator[:, 1]
    inner_real = inner[:, 0]
    inner_imag = inner[:, 1]
    real_part = orbital_product(prop_real, inner_real) - orbital_product(prop_imag, inner_imag)
    imag_part = orbital_product(prop_real, inner_imag) + orbital_product(prop_imag, inner_real)
    return jnp.stack([real_part, imag_part], axis=1)


def second_order(local_green, column):
    green_real = local_green[0]
    green_imag = local_green[1]
    square_real = green_real * green_real - green_imag * green_imag
    square_imag = 2.0 * green_real * green_imag
    real_part = square_real * column[0] - square_imag * column[1]
    imag_part = square_real * column[1] + square_imag * column[0]
    return COUPLING * COUPLING * jnp.stack([real_part, imag_part], axis=0)


def body(green_hist, sigma_hist, prev_row, propagator, impurity_column, sigma_start):
    block_width = prev_row.shape[-1]
    point_count = prev_row.shape[0] * lax.axis_size("ka")
    green_row = prev_row
    self_energy = sigma_start
    for iteration in range(ITERS):
        block = sigma_block(self_energy).astype(jnp.bfloat16)
        partial_terms = jnp.einsum(
            "oarbs,krbcst->koact", block, green_hist, preferred_element_type=jnp.float32
        )
        rows_low = row_block(green_row).astype(jnp.bfloat16)
        partial_terms = partial_terms + jnp.einsum(
            "koarbs,rbcst->koact", rows_low, sigma_hist, preferred_element_type=jnp.float32
        )
        summed = lax.psum(partial_terms, "ta")
        offset = lax.axis_index("ta") * block_width
        convolved = lax.dynamic_slice_in_dim(summed, offset, block_width, 4)
        green_row = propagate(propagator, prev_row + TIME_STEP * convolved)
        own_sum = jnp.sum(green_row, axis=0)
        local_green = lax.psum(own_sum, "ka") / point_count
        self_energy = second_order(local_green, impurity_column)
    return (green_row, self_energy)


def solution(mesh):
    placed = (
        P("ka", None, None, None, "ta", None),
        P(None, None, None, "ta", None),
        P("ka", None, None, None, "ta"),
        P("ka", None, None, None),
        P(None, None, None, "ta"),
        P(None, None, None, "ta"),
    )
    return jax.shard_map(
        body,
        mesh=mesh,
        in_specs=placed,
        out_specs=(P("ka", None, None, None, "ta"), P(None, None, None, "ta")),
        check_vma=False,
    )
```

profile of v0, /device:TPU:64, one launch (start us, length us, event | category | flops | bytes accessed | tf_op | source)
XLA Modules:
  0.0 747.7 jit_solution(10479503619860274841)
XLA Ops:
  0.6 0.0 copy-start.2
  0.6 0.0 copy-start.1
  0.7 0.0 copy-start
  0.7 0.8 slice.57
  1.5 0.8 slice.58
  2.3 0.7 slice_bitcast_fusion.5
  3.0 0.7 fusion.38
  3.7 0.7 copy.84
  4.5 2.0 fusion.6
  6.5 0.0 copy-done.1
  6.5 0.3 fusion.13
  6.7 11.4 %psum.28 = f32[2,2,2,2,512]{4,2,3,0,1:T(2,128)S(1)} all-reduce(f32[2,2,2,2,512]{4,2,3,0,1:T(2,128)S(1)} %fusion.13), channel_id=1, replica_groups=mesh['ka'=128,'ta'=4] {'ta'}, use_global_device_ids=true, to_apply=%region_0.0 | all-reduce | flops 8192 | bytes 65536 | tf_op jit(solution)/shard_map/psum | solution.py:67
  18.2 0.0 copy-done.2
  18.2 0.1 multiply_reduce_fusion.6
  18.4 358.2 %psum.29 = f32[2,2,2,128]{3,1,2,0:T(2,128)S(1)} all-reduce(f32[2,2,2,128]{3,1,2,0:T(2,128)S(1)} %maximum_reduce_fusion), channel_id=1, replica_groups=mesh['ka'=128,'ta'=4] {'ka'}, use_global_device_ids=true, to_apply=%region_6.0 | all-reduce | flops 1024 | bytes 8192 | tf_op jit(solution)/shard_map/psum | solution.py:72
  376.6 0.0 copy-done
  376.6 0.4 fusion.9
  377.0 0.3 fusion.12
  377.3 10.3 %psum.30 = f32[2,2,2,2,512]{4,2,3,0,1:T(2,128)S(1)} all-reduce(f32[2,2,2,2,512]{4,2,3,0,1:T(2,128)S(1)} %fusion.12), channel_id=1, replica_groups=mesh['ka'=128,'ta'=4] {'ta'}, use_global_device_ids=true, to_apply=%region_7.0 | all-reduce | flops 8192 | bytes 65536 | tf_op jit(solution)/shard_map/psum | solution.py:67
  387.6 0.1 multiply_reduce_fusion.3
  387.8 358.7 %psum.31 = f32[2,2,2,128]{3,1,2,0:T(2,128)S(1)} all-reduce(f32[2,2,2,128]{3,1,2,0:T(2,128)S(1)} %copy.88), channel_id=1, replica_groups=mesh['ka'=128,'ta'=4] {'ka'}, use_global_device_ids=true, to_apply=%region_13.0 | all-reduce | flops 1024 | bytes 8192 | tf_op jit(solution)/shard_map/psum | solution.py:72
  746.5 0.6 copy.90
  747.1 0.6 copy.89
  (28 shorter events, 0.2 us)
Async XLA Ops:
  0.6 17.5 %copy-start.2 = (f32[2,2,2,2,128]{4,3,2,1,0:T(2,128)S(1)}, f32[2,2,2,2,128]{4,3,2,1,0:T(2,128)}, u32[]{:S(2)}) copy-start(f32[2,2,2,2,128]{4,3,2,1,0:T(2,128)} %param.8) | copy-start | bytes 24580
  0.6 5.8 copy-start.1
  0.7 376.0 %copy-start = (bf16[2,2,2,2,128,512]{5,4,3,2,1,0:T(8,128)(2,1)S(1)}, bf16[2,2,2,2,128,512]{5,4,3,2,1,0:T(8,128)(2,1)}, u32[]{:S(2)}) copy-start(bf16[2,2,2,2,128,512]{5,4,3,2,1,0:T(8,128)(2,1)} %param.6) | copy-start | bytes 6291460
where the time goes:
time: 748 us
  blocking collectives  739 us (99%)
    psum x2, blocking collectives, body(): local_green = lax.psum(own_sum, 'ka') / point_count  717 us
    psum x2, blocking collectives, body(): summed = lax.psum(partial_terms, 'ta')  21.7 us

commit v1 on v0

--- a/solution.py
+++ b/solution.py
@@ -1,13 +1,19 @@
 import jax
 import jax.numpy as jnp
 from jax import lax
-from jax.sharding import PartitionSpec as P
+from jax.sharding import Mesh, PartitionSpec as P
 
 ITERS = 2
 
 
 TIME_STEP = 0.02
 COUPLING = 1.0
+
+CUT = (("yh", 4), ("yl", 2), ("xh", 2), ("z", 8), ("xl", 2), ("core", 2))
+KA = ("yh", "yl", "xh", "z")
+TA = ("xl", "core")
+NEAR = ("yl", "xh")
+FAR = ("yh", "z")
 
 
 def sigma_block(self_energy):
@@ -50,9 +56,18 @@
     return COUPLING * COUPLING * jnp.stack([real_part, imag_part], axis=0)
 
 
+def spread(blocks, axes):
+    return lax.all_to_all(blocks, axes, 0, 0, tiled=True)
+
+
 def body(green_hist, sigma_hist, prev_row, propagator, impurity_column, sigma_start):
-    block_width = prev_row.shape[-1]
-    point_count = prev_row.shape[0] * lax.axis_size("ka")
+    points, width = prev_row.shape[0], prev_row.shape[-1]
+    times = lax.axis_size(TA)
+    near, far = lax.axis_size(NEAR), lax.axis_size(FAR)
+    point_count = points * lax.axis_size(KA)
+    own_time = jnp.arange(times)[:, None] == lax.axis_index(TA)
+    own_prev = jnp.where(own_time, prev_row[..., None, :], 0.0)
+    own_prev = own_prev.reshape(points, 2, 2, 2, times * width)
     green_row = prev_row
     self_energy = sigma_start
     for iteration in range(ITERS):
@@ -64,29 +79,34 @@
         partial_terms = partial_terms + jnp.einsum(
             "koarbs,rbcst->koact", rows_low, sigma_hist, preferred_element_type=jnp.float32
         )
-        summed = lax.psum(partial_terms, "ta")
-        offset = lax.axis_index("ta") * block_width
-        convolved = lax.dynamic_slice_in_dim(summed, offset, block_width, 4)
-        green_row = propagate(propagator, prev_row + TIME_STEP * convolved)
-        own_sum = jnp.sum(green_row, axis=0)
-        local_green = lax.psum(own_sum, "ka") / point_count
+        share = propagate(propagator, own_prev + TIME_STEP * partial_terms)
+        share = share.reshape(points * 8, times, width).transpose(1, 0, 2)
+        share = jnp.broadcast_to(share[None], (near, times, points * 8, width))
+        got = spread(share.reshape(near * times, points * 8, width), NEAR + TA)
+        got = got.reshape(near, times, points, 8, width)
+        own = lax.dynamic_index_in_dim(got, lax.axis_index(NEAR), 0, keepdims=False)
+        green_row = jnp.sum(own, axis=0).reshape(points, 2, 2, 2, width)
+        near_sum = jnp.sum(got, axis=(0, 1, 2))
+        sums = spread(jnp.broadcast_to(near_sum[None], (far, 8, width)), FAR)
+        local_green = (jnp.sum(sums, axis=0) / point_count).reshape(2, 2, 2, width)
         self_energy = second_order(local_green, impurity_column)
     return (green_row, self_energy)
 
 
 def solution(mesh):
+    fine = Mesh(mesh.devices.reshape([n for _, n in CUT]), [name for name, _ in CUT])
     placed = (
-        P("ka", None, None, None, "ta", None),
-        P(None, None, None, "ta", None),
-        P("ka", None, None, None, "ta"),
-        P("ka", None, None, None),
-        P(None, None, None, "ta"),
-        P(None, None, None, "ta"),
+        P(KA, None, None, None, TA, None),
+        P(None, None, None, TA, None),
+        P(KA, None, None, None, TA),
+        P(KA, None, None, None),
+        P(None, None, None, TA),
+        P(None, None, None, TA),
     )
     return jax.shard_map(
         body,
-        mesh=mesh,
+        mesh=fine,
         in_specs=placed,
-        out_specs=(P("ka", None, None, None, "ta"), P(None, None, None, "ta")),
+        out_specs=(P(KA, None, None, None, TA), P(None, None, None, TA)),
         check_vma=False,
     )

time: 748 us -> 76 us (0.10)
  the two profiles are of different devices: /device:TPU:64 before, /device:TPU:1 now
where the time goes in v1:
time: 76 us; the launch traced here: 75.5 us
  waiting for transfers between devices  28.5 us (38%)
  starting transfers between devices  25.4 us (33%)
  blocking collectives  10.8 us (14%)
  local copies, waits for them, and re-layouts  5.7 us (8%)
  matrix products  2.94 us (4%)
  other arithmetic  1.24 us (2%)
  between operations  1.01 us (1%)
    all_to_all x3, waiting for transfers between devices, spread(): return lax.all_to_all(blocks, axes, 0, 0, tiled=True)  28.5 us
    all_to_all x3, starting transfers between devices, spread(): return lax.all_to_all(blocks, axes, 0, 0, tiled=True)  25.4 us
    all_to_all x1, blocking collectives, spread(): return lax.all_to_all(blocks, axes, 0, 0, tiled=True)  10.8 us
    dot_general x2, matrix products, body(): jnp.einsum('oarbs,krbcst->koact', block, green_hist, preferred_element_ty...  2.39 us
  transfers between devices with their start and end apart: 3, of which 3 were waited for; matrix products, arithmetic and copies ran while one was open for 1% of the time, Pallas kernels for 0%

profile of v1, /device:TPU:1, one launch (start us, length us, event | category | flops | bytes accessed | tf_op | source)
XLA Modules:
  0.0 75.5 jit_solution(2937997398926770916)
XLA Ops:
  0.6 0.0 copy-start.2
  0.6 0.8 %slice.67 = bf16[1,2,2,128]{3,2,1,0:T(2,128)(2,1)S(1)} slice(f32[2,2,2,128]{3,2,1,0:T(2,128)} %param.11), slice={[0:1], [0:2], [0:2], [0:128]} | slice | bytes 2048 | tf_op jit(solution)/shard_map/slice | solution.py:20
  1.4 0.7 slice.68
  2.1 0.7 copy.68
  2.8 0.1 broadcast_bitcast_fusion
  2.9 0.7 slice_bitcast_fusion.4
  3.7 0.0 copy-start.1
  3.7 2.0 %fusion.6 = f32[2,2,2,2,512]{4,2,3,0,1:T(2,128)S(1)} fusion(bf16[2,2,2,2,128,512]{5,4,3,2,1,0:T(8,128)(2,1)} %param.6, bf16[1,2,2,2,128]{4,1,2,3,0:T(2,128)(2,1)S(1)} %get-tuple-element.46, bf16[1,2,2,2,128]{4,1,2,3,0:T(2,128)(2,1)S(1)} %get-tuple-element.45), kind=kOutput, calls=%fused_computation.6 | convolution fusion | flops 8396800 | bytes 2134016 | tf_op jit(solution)/shard_map/oarbs,krbcst->koact/dot_general | solution.py:75
  5.7 0.0 copy-start
  5.7 0.0 copy-done.2
  5.7 0.3 fusion.17
  6.1 0.1 multiply_reduce_fusion.7
  6.3 0.6 broadcast_in_dim.58
  7.0 10.2 %all-to-all-start = ((f32[16,16,128]{2,1,0:T(8,128)}), f32[16,16,128]{2,1,0:T(8,128)S(1)}, u32[]{:S(2)}, u32[]{:S(2)}) async-start(f32[16,16,128]{2,1,0:T(8,128)} %bitcast.30), calls=%async_computation | async-start | bytes 262144 | tf_op jit(solution)/shard_map/all_to_all | solution.py:60
  17.2 0.0 copy-done.1
  17.2 6.2 %all-to-all-done = f32[16,16,128]{2,1,0:T(8,128)S(1)} async-done(((f32[16,16,128]{2,1,0:T(8,128)}), f32[16,16,128]{2,1,0:T(8,128)S(1)}, u32[]{:S(2)}, u32[]{:S(2)}) %all-to-all-start) | async-done | bytes 131104 | tf_op jit(solution)/shard_map/all_to_all | solution.py:60
  23.5 0.6 broadcast_in_dim.59
  24.1 11.4 %all-to-all-start.1 = ((f32[32,8,128]{2,1,0:T(8,128)}), f32[32,8,128]{2,1,0:T(8,128)S(1)}, u32[]{:S(2)}, u32[]{:S(2)}) async-start(f32[32,8,128]{2,1,0:T(8,128)} %broadcast_in_dim.59), calls=%async_computation.1 | async-start | bytes 262144 | tf_op jit(solution)/shard_map/all_to_all | solution.py:60
  35.5 11.4 %all-to-all-done.1 = f32[32,8,128]{2,1,0:T(8,128)S(1)} async-done(((f32[32,8,128]{2,1,0:T(8,128)}), f32[32,8,128]{2,1,0:T(8,128)S(1)}, u32[]{:S(2)}, u32[]{:S(2)}) %all-to-all-start.1) | async-done | bytes 131104 | tf_op jit(solution)/shard_map/all_to_all | solution.py:60
  47.0 0.0 copy-done
  47.0 0.4 fusion.9
  47.4 0.3 fusion.14
  47.8 0.1 multiply_reduce_fusion.3
  48.1 10.8 %all_to_all.20 = f32[16,16,128]{2,1,0:T(8,128)S(1)} all-to-all(f32[16,16,128]{2,1,0:T(8,128)S(1)} %bitcast.168), channel_id=1, replica_groups=mesh['yh'=4,'yl'=2,'xh'=2,'z'=8,'xl'=2,'core'=2] {'yl','xh','xl','core'}, dimensions={0} | all-to-all | bytes 262144 | tf_op jit(solution)/shard_map/all_to_all | solution.py:60
  58.9 0.6 broadcast_in_dim.61
  59.5 3.9 %all-to-all-start.3 = ((f32[32,8,128]{2,1,0:T(8,128)}), f32[32,8,128]{2,1,0:T(8,128)S(1)}, u32[]{:S(2)}, u32[]{:S(2)}) async-start(f32[32,8,128]{2,1,0:T(8,128)} %broadcast_in_dim.61), calls=%async_computation.3 | async-start | bytes 262144 | tf_op jit(solution)/shard_map/all_to_all | solution.py:60
  63.4 0.6 dynamic-slice_reduce_fusion
  64.0 10.9 %all-to-all-done.3 = f32[32,8,128]{2,1,0:T(8,128)S(1)} async-done(((f32[32,8,128]{2,1,0:T(8,128)}), f32[32,8,128]{2,1,0:T(8,128)S(1)}, u32[]{:S(2)}, u32[]{:S(2)}) %all-to-all-start.3) | async-done | bytes 131104 | tf_op jit(solution)/shard_map/all_to_all | solution.py:60
  74.9 0.6 copy.104
  (50 shorter events, 0.6 us)
Async XLA Ops:
  0.6 5.1 %copy-start.2 = (bf16[2,2,2,128,512]{4,3,2,1,0:T(8,128)(2,1)S(1)}, bf16[2,2,2,128,512]{4,3,2,1,0:T(8,128)(2,1)}, u32[]{:S(2)}) copy-start(bf16[2,2,2,128,512]{4,3,2,1,0:T(8,128)(2,1)} %param.7) | copy-start | bytes 3145732
  3.7 13.5 %copy-start.1 = (f32[2,2,2,128]{3,2,1,0:T(2,128)S(1)}, f32[2,2,2,128]{3,2,1,0:T(2,128)}, u32[]{:S(2)}) copy-start(f32[2,2,2,128]{3,2,1,0:T(2,128)} %param.10) | copy-start | bytes 12292
  5.7 41.3 %copy-start = (bf16[2,2,2,2,128,512]{5,4,3,2,1,0:T(8,128)(2,1)S(1)}, bf16[2,2,2,2,128,512]{5,4,3,2,1,0:T(8,128)(2,1)}, u32[]{:S(2)}) copy-start(bf16[2,2,2,2,128,512]{5,4,3,2,1,0:T(8,128)(2,1)} %param.6) | copy-start | bytes 6291460
  7.0 16.4 %all-to-all-start = ((f32[16,16,128]{2,1,0:T(8,128)}), f32[16,16,128]{2,1,0:T(8,128)S(1)}, u32[]{:S(2)}, u32[]{:S(2)}) async-start(f32[16,16,128]{2,1,0:T(8,128)} %bitcast.30), calls=%async_computation | async-start | bytes 262144 | tf_op jit(solution)/shard_map/all_to_all | solution.py:60
  24.1 22.8 %all-to-all-start.1 = ((f32[32,8,128]{2,1,0:T(8,128)}), f32[32,8,128]{2,1,0:T(8,128)S(1)}, u32[]{:S(2)}, u32[]{:S(2)}) async-start(f32[32,8,128]{2,1,0:T(8,128)} %broadcast_in_dim.59), calls=%async_computation.1 | async-start | bytes 262144 | tf_op jit(solution)/shard_map/all_to_all | solution.py:60
  59.5 15.3 %all-to-all-start.3 = ((f32[32,8,128]{2,1,0:T(8,128)}), f32[32,8,128]{2,1,0:T(8,128)S(1)}, u32[]{:S(2)}, u32[]{:S(2)}) async-start(f32[32,8,128]{2,1,0:T(8,128)} %broadcast_in_dim.61), calls=%async_computation.3 | async-start | bytes 262144 | tf_op jit(solution)/shard_map/all_to_all | solution.py:60

commit v2 on v1

v2 whole, which is shorter than its diff:
```python
import functools

import jax
import jax.numpy as jnp
from jax import lax
from jax.experimental import pallas as pl
from jax.experimental.pallas import tpu as pltpu
from jax.sharding import Mesh, PartitionSpec as P

ITERS = 2


TIME_STEP = 0.02
COUPLING = 1.0

CUT = (("yh", 4), ("yl", 2), ("xh", 2), ("z", 8), ("xl", 2), ("core", 2))
KA = ("yh", "yl", "xh", "z")
TA = ("xl", "core")
NEAR = ("yl", "xh")
FAR = ("yh", "z")


def second_order(local_green, column):
    green_real = local_green[0]
    green_imag = local_green[1]
    square_real = green_real * green_real - green_imag * green_imag
    square_imag = 2.0 * green_real * green_imag
    real_part = square_real * column[0] - square_imag * column[1]
    imag_part = square_real * column[1] + square_imag * column[0]
    return COUPLING * COUPLING * jnp.stack([real_part, imag_part], axis=0)


def spread(blocks, axes):
    return lax.all_to_all(blocks, axes, 0, 0, tiled=True)


def parts_of(ref, index, o, r, b):
    part = ref[(*index, pl.ds(b, 1), slice(None))]
    return -part if (o == 0 and r == 1) else part


def fill_left(sigma_ref, row_ref, sigma_lhs, row_lhs):
    points, width = row_ref.shape[0], row_ref.shape[-1]
    sigma_lhs[...] = jnp.zeros_like(sigma_lhs)
    row_lhs[...] = jnp.zeros_like(row_lhs)
    for o in range(2):
        for a in range(2):
            for j in range(4):
                r, b = j // 2, j % 2
                lanes = pl.ds(j * width, width)
                part = parts_of(sigma_ref, (o ^ r, a), o, r, b)
                for c in range(2):
                    sigma_lhs[c, pl.ds(c * 4 + o * 2 + a, 1), lanes] = part
                for k in range(points):
                    part = parts_of(row_ref, (k, o ^ r, a), o, r, b)
                    for c in range(2):
                        row_lhs[c, pl.ds(k * 8 + c * 4 + o * 2 + a, 1), lanes] = part


def contract(left, blocks):
    total = None
    for c in range(2):
        right = jnp.concatenate([blocks[j][c] for j in range(4)], axis=0)
        term = jnp.dot(left[c].astype(jnp.bfloat16), right, preferred_element_type=jnp.float32)
        total = term if total is None else total + term
    return total


def propagate_share(near, times, k, inner, prev, factors, out_ref):
    width = prev.shape[-1]
    place = lax.broadcasted_iota(jnp.int32, (8, width), 0)
    own_time = lax.axis_index(TA)
    for t in range(times):
        part = TIME_STEP * inner[:, t * width:(t + 1) * width]
        part = part + jnp.where(own_time == t, prev, 0.0)
        share = None
        for j in range(4):
            low = jnp.broadcast_to(part[j:j + 1], (8, width))
            high = jnp.broadcast_to(part[4 + j:5 + j], (8, width))
            term = factors[j] * jnp.where(place < 4, low, high)
            share = term if share is None else share + term
        for n in range(near):
            for c in range(2):
                out_ref[n * times + t, pl.ds(k * 8 + c, 4, stride=2), :] = share[c * 4:(c + 1) * 4]


def first_kernel(
    near, times,
    prop_in, sigma_in, prev_in, green_in, hist_in,
    out_ref, factor_ref, own_prev, green_buf, hist_buf,
    prop_ref, sigma_ref, prev_ref, sigma_lhs, row_lhs, small, sems,
):
    points, width = prev_ref.shape[0], prev_ref.shape[-1]
    little = [
        pltpu.make_async_copy(src, dst, small.at[i])
        for i, (src, dst) in enumerate(((sigma_in, sigma_ref), (prev_in, prev_ref), (prop_in, prop_ref)))
    ]
    for copy in little:
        copy.start()
    large = {}
    for j in range(4):
        large[points, j] = pltpu.make_async_copy(hist_in.at[j // 2, j % 2], hist_buf.at[j], sems.at[points, j])
        large[points, j].start()
    for k in range(points):
        for j in range(4):
            large[k, j] = pltpu.make_async_copy(green_in.at[k, j // 2, j % 2], green_buf.at[k, j], sems.at[k, j])
            large[k, j].start()
    for copy in little:
        copy.wait()
    fill_left(sigma_ref, prev_ref, sigma_lhs, row_lhs)
    for k in range(points):
        for o in range(2):
            for a in range(2):
                for c in range(2):
                    own_prev[pl.ds(k * 8 + c * 4 + o * 2 + a, 1), :] = prev_ref[k, o, a, pl.ds(c, 1), :]
    for k in range(points):
        for r in range(2):
            for a in range(2):
                for b in range(2):
                    entry = jnp.broadcast_to(prop_ref[k, r, pl.ds(a, 1), pl.ds(b, 1)], (1, width))
                    for o in range(2):
                        value = -entry if (o == 1 and r == 1) else entry
                        for c in range(2):
                            factor_ref[k, o * 2 + b, pl.ds(c * 4 + (o ^ r) * 2 + a, 1), :] = value
    for j in range(4):
        large[points, j].wait()
    row_terms = contract(row_lhs, [[hist_buf[j, c] for c in range(2)] for j in range(4)])
    for k in range(points):
        for j in range(4):
            large[k, j].wait()
        inner = contract(sigma_lhs, [[green_buf[k, j, c] for c in range(2)] for j in range(4)])
        inner = inner + row_terms[k * 8:(k + 1) * 8]
        factors = [factor_ref[k, j] for j in range(4)]
        propagate_share(near, times, k, inner, own_prev[pl.ds(k * 8, 8), :], factors, out_ref)


def next_kernel(
    near, times,
    sigma_ref, row_ref, factor_ref, own_prev, green_ref, hist_ref, out_ref,
    sigma_lhs, row_lhs,
):
    points = row_ref.shape[0]
    fill_left(sigma_ref, row_ref, sigma_lhs, row_lhs)
    row_terms = contract(row_lhs, [[hist_ref[j, c] for c in range(2)] for j in range(4)])
    for k in range(points):
        inner = contract(sigma_lhs, [[green_ref[k, j, c] for c in range(2)] for j in range(4)])
        inner = inner + row_terms[k * 8:(k + 1) * 8]
        factors = [factor_ref[k, j] for j in range(4)]
        propagate_share(near, times, k, inner, own_prev[pl.ds(k * 8, 8), :], factors, out_ref)


VMEM = pl.BlockSpec(memory_space=pltpu.VMEM)
HBM = pl.BlockSpec(memory_space=pltpu.HBM)


def left_scratch(points, width):
    return [
        pltpu.VMEM((2, 8, 4 * width), jnp.float32),
        pltpu.VMEM((2, points * 8, 4 * width), jnp.float32),
    ]


def first_share(propagator, self_energy, prev_row, green_hist, sigma_hist, near, times):
    points, width = prev_row.shape[0], prev_row.shape[-1]
    full = sigma_hist.shape[-1]
    return pl.pallas_call(
        functools.partial(first_kernel, near, times),
        out_shape=(
            jax.ShapeDtypeStruct((near * times, points * 8, width), jnp.float32),
            jax.ShapeDtypeStruct((points, 4, 8, width), jnp.float32),
            jax.ShapeDtypeStruct((points * 8, width), jnp.float32),
            jax.ShapeDtypeStruct((points, 4, 2, width, full), jnp.bfloat16),
            jax.ShapeDtypeStruct((4, 2, width, full), jnp.bfloat16),
        ),
        in_specs=[HBM] * 5,
        out_specs=(VMEM,) * 5,
        scratch_shapes=[
            pltpu.VMEM(propagator.shape, jnp.float32),
            pltpu.VMEM(self_energy.shape, jnp.float32),
            pltpu.VMEM(prev_row.shape, jnp.float32),
            *left_scratch(points, width),
            pltpu.SemaphoreType.DMA((3,)),
            pltpu.SemaphoreType.DMA((points + 1, 4)),
        ],
        compiler_params=pltpu.CompilerParams(vmem_limit_bytes=16 << 20),
        name="first_share",
    )(*(
        pltpu.with_memory_space_constraint(x, pltpu.HBM)
        for x in (propagator, self_energy, prev_row, green_hist, sigma_hist)
    ))


def next_share(self_energy, green_row, factors, own_prev, green_hist, sigma_hist, near, times):
    points, width = green_row.shape[0], green_row.shape[-1]
    return pl.pallas_call(
        functools.partial(next_kernel, near, times),
        out_shape=jax.ShapeDtypeStruct((near * times, points * 8, width), jnp.float32),
        in_specs=[VMEM] * 6,
        out_specs=VMEM,
        scratch_shapes=left_scratch(points, width),
        compiler_params=pltpu.CompilerParams(vmem_limit_bytes=16 << 20),
        name="next_share",
    )(self_energy, green_row, factors, own_prev, green_hist, sigma_hist)


def body(green_hist, sigma_hist, prev_row, propagator, impurity_column, sigma_start):
    points, width = prev_row.shape[0], prev_row.shape[-1]
    times = lax.axis_size(TA)
    near, far = lax.axis_size(NEAR), lax.axis_size(FAR)
    point_count = points * lax.axis_size(KA)
    place = lax.axis_index(NEAR)
    column = impurity_column
    for iteration in range(ITERS):
        if iteration == 0:
            share, factors, own_prev, green_held, hist_held = first_share(
                propagator, sigma_start, prev_row, green_hist, sigma_hist, near, times
            )
        else:
            share = next_share(
                self_energy, green_row, factors, own_prev, green_held, hist_held, near, times
            )
        share, place = lax.optimization_barrier((share, place))
        got = spread(share, NEAR + TA)
        got, column = lax.optimization_barrier((got, column))
        got = got.reshape(near, times, points, 8, width)
        own = lax.dynamic_index_in_dim(got, place, 0, keepdims=False, allow_negative_indices=False)
        green_row = jnp.sum(own, axis=0).reshape(points, 2, 2, 2, width)
        near_sum = jnp.sum(got, axis=(0, 1, 2))
        near_sum, green_row = lax.optimization_barrier((near_sum, green_row))
        sums = spread(jnp.broadcast_to(near_sum[None], (far, 8, width)), FAR)
        sums, green_row = lax.optimization_barrier((sums, green_row))
        local_green = (jnp.sum(sums, axis=0) / point_count).reshape(2, 2, 2, width)
        self_energy = second_order(local_green, column)
    return (green_row, self_energy)


def solution(mesh):
    fine = Mesh(mesh.devices.reshape([n for _, n in CUT]), [name for name, _ in CUT])
    placed = (
        P(KA, None, None, None, TA, None),
        P(None, None, None, TA, None),
        P(KA, None, None, None, TA),
        P(KA, None, None, None),
        P(None, None, None, TA),
        P(None, None, None, TA),
    )
    return jax.shard_map(
        body,
        mesh=fine,
        in_specs=placed,
        out_specs=(P(KA, None, None, None, TA), P(None, None, None, TA)),
        check_vma=False,
    )
```

time: 76 us -> 69.6 us (0.916)
  blocking collectives: 10.8 us -> 64 us
  waiting for transfers between devices: 28.5 us -> 0 us
  starting transfers between devices: 25.4 us -> 0 us
  local copies, waits for them, and re-layouts: 5.7 us -> 0.02 us
  Pallas kernels: 0 us -> 3.23 us
  matrix products: 2.94 us -> 0 us
    all_to_all x1 -> x4, blocking collectives: 10.8 us -> 64 us  [spread(): return lax.all_to_all(blocks, axes, 0, 0, tiled=True)]
    all_to_all x3 -> x0, waiting for transfers between devices: 28.5 us -> none  [spread(): return lax.all_to_all(blocks, axes, 0, 0, tiled=True)]
    all_to_all x3 -> x0, starting transfers between devices: 25.4 us -> none  [spread(): return lax.all_to_all(blocks, axes, 0, 0, tiled=True)]
    pallas_call x0 -> x2, Pallas kernels: none -> 3.23 us  [the longest x1 2.68 us: first_share(): pl.pallas_call(functools.partial(first_kernel, near, times), out_shape=(j...]
    dot_general x4 -> x0, matrix products: 2.94 us -> none  [the longest x2 2.39 us: body(): jnp.einsum('oarbs,krbcst->koact', block, green_hist, preferred_element_ty...]
    slice x5 -> x0, local copies, waits for them, and re-layouts: 1.47 us -> none  [the longest x1 0.77 us: sigma_block(): real_part = self_energy[0]]
    unnamed x10 -> x2, local copies, waits for them, and re-layouts: 1.32 us -> 0.01 us
    broadcast_in_dim x2, local copies, waits for them, and re-layouts: 1.29 us -> 0.02 us  [body(): sums = spread(jnp.broadcast_to(near_sum[None], (far, 8, width)), FAR)]
  transfers between devices with their start and end apart: 3 -> 0, of which waited for: 3 -> 0; matrix products, arithmetic and copies ran while one was open for 1% -> 0% of each run, Pallas kernels for 0% -> 0%
where the time goes in v2:
time: 69.6 us; the launch traced here: 69.4 us
  blocking collectives  64 us (92%)
  Pallas kernels  3.23 us (5%)
  other arithmetic  1.39 us (2%)
  between operations  0.74 us (1%)
    all_to_all x4, blocking collectives, spread(): return lax.all_to_all(blocks, axes, 0, 0, tiled=True)  64 us
    pallas_call x1, Pallas kernels, first_share(): pl.pallas_call(functools.partial(first_kernel, near, times), out_shape=(j...  2.68 us

profile of v2, /device:TPU:1, one launch (start us, length us, event | category | flops | bytes accessed | tf_op | source)
XLA Modules:
  0.0 69.4 jit_solution(11468596200990925248)
XLA Ops:
  0.6 0.0 copy-start
  0.6 2.7 %first_share.1 = (f32[16,16,128]{2,1,0:T(8,128)S(1)}, f32[2,4,8,128]{3,2,1,0:T(8,128)S(1)}, f32[16,128]{1,0:T(8,128)S(1)}, bf16[2,4,2,128,512]{4,3,2,1,0:T(8,128)(2,1)S(1)}, bf16[4,2,128,512]{3,2,1,0:T(8,128)(2,1)S(1)}) custom-call(f32[2,2,2,2]{3,2,1,0:T(2,128)} %prop_in.1, f32[2,2,2,128]{3,2,1,0:T(2,128)} %sigma_in.1, f32[2,2,2,2,128]{4,3,2,1,0:T(2,128)} %prev_in.1, ...), custom_call_target="tpu_custom_call" | custom-call | tf_op jit(solution)/shard_map/first_share/pallas_call | solution.py:166
  3.3 15.5 %all_to_all.20 = f32[16,16,128]{2,1,0:T(8,128)S(1)} all-to-all(f32[16,16,128]{2,1,0:T(8,128)S(1)} %get-tuple-element.24), channel_id=1, replica_groups=mesh['yh'=4,'yl'=2,'xh'=2,'z'=8,'xl'=2,'core'=2] {'yl','xh','xl','core'}, dimensions={0} | all-to-all | bytes 262144 | tf_op jit(solution)/shard_map/all_to_all | solution.py:34
  18.9 23.3 %all_to_all.21 = f32[32,8,128]{2,1,0:T(8,128)S(1)} all-to-all(f32[32,8,128]{2,1,0:T(8,128)S(1)} %broadcast_in_dim.4), channel_id=1, replica_groups=mesh['yh'=4,'yl'=2,'xh'=2,'z'=8,'xl'=2,'core'=2] {'yh','z'}, dimensions={0} | all-to-all | bytes 262144 | tf_op jit(solution)/shard_map/all_to_all | solution.py:34
  42.3 0.0 copy-done
  42.3 0.5 next_share.1
  42.9 10.8 %all_to_all.22 = f32[16,16,128]{2,1,0:T(8,128)S(1)} all-to-all(f32[16,16,128]{2,1,0:T(8,128)S(1)} %next_share.1), channel_id=1, replica_groups=mesh['yh'=4,'yl'=2,'xh'=2,'z'=8,'xl'=2,'core'=2] {'yl','xh','xl','core'}, dimensions={0} | all-to-all | bytes 262144 | tf_op jit(solution)/shard_map/all_to_all | solution.py:34
  53.7 0.6 dynamic-slice_reduce_fusion
  54.3 14.4 %all_to_all.23 = f32[32,8,128]{2,1,0:T(8,128)S(1)} all-to-all(f32[32,8,128]{2,1,0:T(8,128)S(1)} %broadcast_in_dim.5), channel_id=1, replica_groups=mesh['yh'=4,'yl'=2,'xh'=2,'z'=8,'xl'=2,'core'=2] {'yh','z'}, dimensions={0} | all-to-all | bytes 262144 | tf_op jit(solution)/shard_map/all_to_all | solution.py:34
  68.8 0.6 pad_maximum_fusion.1
  (16 shorter events, 0.2 us)
Async XLA Ops:
  0.6 41.6 %copy-start = (f32[2,2,2,128]{3,2,1,0:T(2,128)S(1)}, f32[2,2,2,128]{3,2,1,0:T(2,128)}, u32[]{:S(2)}) copy-start(f32[2,2,2,128]{3,2,1,0:T(2,128)} %param.10) | copy-start | bytes 12292

commit v3 on v2

--- a/solution.py
+++ b/solution.py
@@ -27,7 +27,7 @@
     square_imag = 2.0 * green_real * green_imag
     real_part = square_real * column[0] - square_imag * column[1]
     imag_part = square_real * column[1] + square_imag * column[0]
-    return COUPLING * COUPLING * jnp.stack([real_part, imag_part], axis=0)
+    return COUPLING * COUPLING * real_part, COUPLING * COUPLING * imag_part
 
 
 def spread(blocks, axes):
@@ -104,7 +104,7 @@
     for k in range(points):
         for j in range(4):
             large[k, j] = pltpu.make_async_copy(green_in.at[k, j // 2, j % 2], green_buf.at[k, j], sems.at[k, j])
-            large[k, j].start()
+            large[k, j].start(priority=1)
     for copy in little:
         copy.wait()
     fill_left(sigma_ref, prev_ref, sigma_lhs, row_lhs)
@@ -147,6 +147,23 @@
         inner = inner + row_terms[k * 8:(k + 1) * 8]
         factors = [factor_ref[k, j] for j in range(4)]
         propagate_share(near, times, k, inner, own_prev[pl.ds(k * 8, 8), :], factors, out_ref)
+
+
+def last_kernel(
+    point_count, sums_ref, row_ref, column_ref, row_out, energy_out, energy_ref, local_ref, sems,
+):
+    row_copy = pltpu.make_async_copy(row_ref, row_out, sems.at[0])
+    row_copy.start()
+    local_ref[...] = jnp.sum(sums_ref[...], axis=0) / point_count
+    for a in range(2):
+        local = [local_ref[pl.ds(o * 4 + a * 2, 2), :] for o in range(2)]
+        parts = second_order(local, [column_ref[o, a] for o in range(2)])
+        for o in range(2):
+            energy_ref[o, a] = parts[o]
+    energy_copy = pltpu.make_async_copy(energy_ref, energy_out, sems.at[1])
+    energy_copy.start()
+    row_copy.wait()
+    energy_copy.wait()
 
 
 VMEM = pl.BlockSpec(memory_space=pltpu.VMEM)
@@ -203,6 +220,25 @@
     )(self_energy, green_row, factors, own_prev, green_hist, sigma_hist)
 
 
+def last_step(sums, green_row, column, point_count):
+    return pl.pallas_call(
+        functools.partial(last_kernel, point_count),
+        out_shape=(
+            jax.ShapeDtypeStruct(green_row.shape, jnp.float32),
+            jax.ShapeDtypeStruct(column.shape, jnp.float32),
+        ),
+        in_specs=[VMEM] * 3,
+        out_specs=(HBM,) * 2,
+        scratch_shapes=[
+            pltpu.VMEM(column.shape, jnp.float32),
+            pltpu.VMEM(sums.shape[1:], jnp.float32),
+            pltpu.SemaphoreType.DMA((2,)),
+        ],
+        compiler_params=pltpu.CompilerParams(vmem_limit_bytes=16 << 20),
+        name="last_step",
+    )(sums, green_row, column)
+
+
 def body(green_hist, sigma_hist, prev_row, propagator, impurity_column, sigma_start):
     points, width = prev_row.shape[0], prev_row.shape[-1]
     times = lax.axis_size(TA)
@@ -229,9 +265,10 @@
         near_sum, green_row = lax.optimization_barrier((near_sum, green_row))
         sums = spread(jnp.broadcast_to(near_sum[None], (far, 8, width)), FAR)
         sums, green_row = lax.optimization_barrier((sums, green_row))
+        if iteration == ITERS - 1:
+            return last_step(sums, green_row, column, point_count)
         local_green = (jnp.sum(sums, axis=0) / point_count).reshape(2, 2, 2, width)
-        self_energy = second_order(local_green, column)
-    return (green_row, self_energy)
+        self_energy = jnp.stack(second_order(local_green, column), axis=0)
 
 
 def solution(mesh):

time: 69.6 us -> 68.6 us (0.986)
  other arithmetic: 1.39 us -> 0.14 us
where the time goes in v3:
time: 68.6 us; the launch traced here: 68.3 us
  blocking collectives  64 us (93%)
  Pallas kernels  3.43 us (5%)
  between operations  0.74 us (1%)
    all_to_all x4, blocking collectives, spread(): return lax.all_to_all(blocks, axes, 0, 0, tiled=True)  64 us
    pallas_call x1, Pallas kernels, first_share(): pl.pallas_call(functools.partial(first_kernel, near, times), out_shape=(j...  2.23 us

profile of v3, /device:TPU:1, one launch (start us, length us, event | category | flops | bytes accessed | tf_op | source)
XLA Modules:
  0.0 68.3 jit_solution(11375706001419069535)
XLA Ops:
  0.6 0.0 copy-start
  0.6 2.2 %first_share.1 = (f32[16,16,128]{2,1,0:T(8,128)S(1)}, f32[2,4,8,128]{3,2,1,0:T(8,128)S(1)}, f32[16,128]{1,0:T(8,128)S(1)}, bf16[2,4,2,128,512]{4,3,2,1,0:T(8,128)(2,1)S(1)}, bf16[4,2,128,512]{3,2,1,0:T(8,128)(2,1)S(1)}) custom-call(f32[2,2,2,2]{3,2,1,0:T(2,128)} %prop_in.1, f32[2,2,2,128]{3,2,1,0:T(2,128)} %sigma_in.1, f32[2,2,2,2,128]{4,3,2,1,0:T(2,128)} %prev_in.1, ...), custom_call_target="tpu_custom_call" | custom-call | tf_op jit(solution)/shard_map/first_share/pallas_call | solution.py:183
  2.9 15.5 %all_to_all.20 = f32[16,16,128]{2,1,0:T(8,128)S(1)} all-to-all(f32[16,16,128]{2,1,0:T(8,128)S(1)} %get-tuple-element.24), channel_id=1, replica_groups=mesh['yh'=4,'yl'=2,'xh'=2,'z'=8,'xl'=2,'core'=2] {'yl','xh','xl','core'}, dimensions={0} | all-to-all | bytes 262144 | tf_op jit(solution)/shard_map/all_to_all | solution.py:34
  18.5 23.3 %all_to_all.21 = f32[32,8,128]{2,1,0:T(8,128)S(1)} all-to-all(f32[32,8,128]{2,1,0:T(8,128)S(1)} %broadcast_in_dim.4), channel_id=1, replica_groups=mesh['yh'=4,'yl'=2,'xh'=2,'z'=8,'xl'=2,'core'=2] {'yh','z'}, dimensions={0} | all-to-all | bytes 262144 | tf_op jit(solution)/shard_map/all_to_all | solution.py:34
  41.8 0.0 copy-done
  41.9 0.5 next_share.1
  42.4 10.8 %all_to_all.22 = f32[16,16,128]{2,1,0:T(8,128)S(1)} all-to-all(f32[16,16,128]{2,1,0:T(8,128)S(1)} %next_share.1), channel_id=1, replica_groups=mesh['yh'=4,'yl'=2,'xh'=2,'z'=8,'xl'=2,'core'=2] {'yl','xh','xl','core'}, dimensions={0} | all-to-all | bytes 262144 | tf_op jit(solution)/shard_map/all_to_all | solution.py:34
  53.3 14.4 %all_to_all.23.sums_ref = f32[32,8,128]{2,1,0:T(8,128)S(1)} all-to-all(f32[32,8,128]{2,1,0:T(8,128)S(1)} %broadcast_in_dim.5), channel_id=1, replica_groups=mesh['yh'=4,'yl'=2,'xh'=2,'z'=8,'xl'=2,'core'=2] {'yh','z'}, dimensions={0} | all-to-all | bytes 262144 | tf_op jit(solution)/shard_map/all_to_all | solution.py:34
  67.7 0.7 last_step.1
  (13 shorter events, 0.2 us)
Async XLA Ops:
  0.6 41.2 %copy-start = (f32[2,2,2,128]{3,2,1,0:T(2,128)S(1)}, f32[2,2,2,128]{3,2,1,0:T(2,128)}, u32[]{:S(2)}) copy-start(f32[2,2,2,128]{3,2,1,0:T(2,128)} %column_ref) | copy-start | bytes 12292

commit v4 on v3

--- a/solution.py
+++ b/solution.py
@@ -18,6 +18,8 @@
 TA = ("xl", "core")
 NEAR = ("yl", "xh")
 FAR = ("yh", "z")
+NEAR_FIRST = (0, 0)
+FAR_FIRST = (22, 22)
 
 
 def second_order(local_green, column):
@@ -30,8 +32,9 @@
     return COUPLING * COUPLING * real_part, COUPLING * COUPLING * imag_part
 
 
-def spread(blocks, axes):
-    return lax.all_to_all(blocks, axes, 0, 0, tiled=True)
+def spread(blocks, axes, first):
+    order = [rank ^ first for rank in range(lax.axis_size(axes))]
+    return lax.all_to_all(blocks, axes, 0, 0, tiled=True, axis_index_groups=[order])
 
 
 def parts_of(ref, index, o, r, b):
@@ -66,7 +69,7 @@
     return total
 
 
-def propagate_share(near, times, k, inner, prev, factors, out_ref):
+def propagate_share(near, times, first, k, inner, prev, factors, out_ref):
     width = prev.shape[-1]
     place = lax.broadcasted_iota(jnp.int32, (8, width), 0)
     own_time = lax.axis_index(TA)
@@ -81,11 +84,11 @@
             share = term if share is None else share + term
         for n in range(near):
             for c in range(2):
-                out_ref[n * times + t, pl.ds(k * 8 + c, 4, stride=2), :] = share[c * 4:(c + 1) * 4]
+                out_ref[n * times + (t ^ first), pl.ds(k * 8 + c, 4, stride=2), :] = share[c * 4:(c + 1) * 4]
 
 
 def first_kernel(
-    near, times,
+    near, times, first,
     prop_in, sigma_in, prev_in, green_in, hist_in,
     out_ref, factor_ref, own_prev, green_buf, hist_buf,
     prop_ref, sigma_ref, prev_ref, sigma_lhs, row_lhs, small, sems,
@@ -131,11 +134,11 @@
         inner = contract(sigma_lhs, [[green_buf[k, j, c] for c in range(2)] for j in range(4)])
         inner = inner + row_terms[k * 8:(k + 1) * 8]
         factors = [factor_ref[k, j] for j in range(4)]
-        propagate_share(near, times, k, inner, own_prev[pl.ds(k * 8, 8), :], factors, out_ref)
+        propagate_share(near, times, first, k, inner, own_prev[pl.ds(k * 8, 8), :], factors, out_ref)
 
 
 def next_kernel(
-    near, times,
+    near, times, first,
     sigma_ref, row_ref, factor_ref, own_prev, green_ref, hist_ref, out_ref,
     sigma_lhs, row_lhs,
 ):
@@ -146,7 +149,7 @@
         inner = contract(sigma_lhs, [[green_ref[k, j, c] for c in range(2)] for j in range(4)])
         inner = inner + row_terms[k * 8:(k + 1) * 8]
         factors = [factor_ref[k, j] for j in range(4)]
-        propagate_share(near, times, k, inner, own_prev[pl.ds(k * 8, 8), :], factors, out_ref)
+        propagate_share(near, times, first, k, inner, own_prev[pl.ds(k * 8, 8), :], factors, out_ref)
 
 
 def last_kernel(
@@ -177,11 +180,11 @@
     ]
 
 
-def first_share(propagator, self_energy, prev_row, green_hist, sigma_hist, near, times):
+def first_share(propagator, self_energy, prev_row, green_hist, sigma_hist, near, times, first):
     points, width = prev_row.shape[0], prev_row.shape[-1]
     full = sigma_hist.shape[-1]
     return pl.pallas_call(
-        functools.partial(first_kernel, near, times),
+        functools.partial(first_kernel, near, times, first),
         out_shape=(
             jax.ShapeDtypeStruct((near * times, points * 8, width), jnp.float32),
             jax.ShapeDtypeStruct((points, 4, 8, width), jnp.float32),
@@ -207,10 +210,10 @@
     ))
 
 
-def next_share(self_energy, green_row, factors, own_prev, green_hist, sigma_hist, near, times):
+def next_share(self_energy, green_row, factors, own_prev, green_hist, sigma_hist, near, times, first):
     points, width = green_row.shape[0], green_row.shape[-1]
     return pl.pallas_call(
-        functools.partial(next_kernel, near, times),
+        functools.partial(next_kernel, near, times, first),
         out_shape=jax.ShapeDtypeStruct((near * times, points * 8, width), jnp.float32),
         in_specs=[VMEM] * 6,
         out_specs=VMEM,
@@ -247,23 +250,24 @@
     place = lax.axis_index(NEAR)
     column = impurity_column
     for iteration in range(ITERS):
+        first = NEAR_FIRST[iteration] % times
         if iteration == 0:
             share, factors, own_prev, green_held, hist_held = first_share(
-                propagator, sigma_start, prev_row, green_hist, sigma_hist, near, times
+                propagator, sigma_start, prev_row, green_hist, sigma_hist, near, times, first
             )
         else:
             share = next_share(
-                self_energy, green_row, factors, own_prev, green_held, hist_held, near, times
+                self_energy, green_row, factors, own_prev, green_held, hist_held, near, times, first
             )
         share, place = lax.optimization_barrier((share, place))
-        got = spread(share, NEAR + TA)
+        got = spread(share, NEAR + TA, NEAR_FIRST[iteration])
         got, column = lax.optimization_barrier((got, column))
         got = got.reshape(near, times, points, 8, width)
-        own = lax.dynamic_index_in_dim(got, place, 0, keepdims=False, allow_negative_indices=False)
+        own = lax.dynamic_index_in_dim(got, place ^ (NEAR_FIRST[iteration] // times), 0, keepdims=False, allow_negative_indices=False)
         green_row = jnp.sum(own, axis=0).reshape(points, 2, 2, 2, width)
         near_sum = jnp.sum(got, axis=(0, 1, 2))
         near_sum, green_row = lax.optimization_barrier((near_sum, green_row))
-        sums = spread(jnp.broadcast_to(near_sum[None], (far, 8, width)), FAR)
+        sums = spread(jnp.broadcast_to(near_sum[None], (far, 8, width)), FAR, FAR_FIRST[iteration])
         sums, green_row = lax.optimization_barrier((sums, green_row))
         if iteration == ITERS - 1:
             return last_step(sums, green_row, column, point_count)

time: 68.6 us -> 63.4 us (0.924)
  blocking collectives: 64 us -> 58.8 us
    all_to_all x4, blocking collectives: 64 us -> 58.8 us  [spread(): lax.all_to_all(blocks, axes, 0, 0, tiled=True, axis_index_groups=[order])]
where the time goes in v4:
time: 63.4 us; the launch traced here: 63.1 us
  blocking collectives  58.8 us (93%)
  Pallas kernels  3.43 us (5%)
  between operations  0.74 us (1%)
    all_to_all x4, blocking collectives, spread(): lax.all_to_all(blocks, axes, 0, 0, tiled=True, axis_index_groups=[order])  58.8 us
    pallas_call x1, Pallas kernels, first_share(): pl.pallas_call(functools.partial(first_kernel, near, times, first), out_s...  2.23 us

profile of v4, /device:TPU:1, one launch (start us, length us, event | category | flops | bytes accessed | tf_op | source)
XLA Modules:
  0.0 63.1 jit_solution(2516244573652225673)
XLA Ops:
  0.6 0.0 copy-start
  0.6 2.2 %first_share.1 = (f32[16,16,128]{2,1,0:T(8,128)S(1)}, f32[2,4,8,128]{3,2,1,0:T(8,128)S(1)}, f32[16,128]{1,0:T(8,128)S(1)}, bf16[2,4,2,128,512]{4,3,2,1,0:T(8,128)(2,1)S(1)}, bf16[4,2,128,512]{3,2,1,0:T(8,128)(2,1)S(1)}) custom-call(f32[2,2,2,2]{3,2,1,0:T(2,128)} %prop_in.1, f32[2,2,2,128]{3,2,1,0:T(2,128)} %sigma_in.1, f32[2,2,2,2,128]{4,3,2,1,0:T(2,128)} %prev_in.1, ...), custom_call_target="tpu_custom_call" | custom-call | tf_op jit(solution)/shard_map/first_share/pallas_call | solution.py:186
  2.9 15.5 %all_to_all.20 = f32[16,16,128]{2,1,0:T(8,128)S(1)} all-to-all(f32[16,16,128]{2,1,0:T(8,128)S(1)} %get-tuple-element.24), channel_id=1, replica_groups={{0,1,2,3,32,33,34,35,64,65,66,67,96,97,98,99},{4,5,6,7,36,37,38,39,68,6..., dimensions={0} | all-to-all | bytes 262144 | tf_op jit(solution)/shard_map/all_to_all | solution.py:37
  18.5 18.1 %all_to_all.21 = f32[32,8,128]{2,1,0:T(8,128)S(1)} all-to-all(f32[32,8,128]{2,1,0:T(8,128)S(1)} %broadcast_in_dim.4), channel_id=1, replica_groups={{280,284,272,276,264,268,256,260,408,412,400,404,392,396,384,388,24,28,..., dimensions={0} | all-to-all | bytes 262144 | tf_op jit(solution)/shard_map/all_to_all | solution.py:37
  36.6 0.0 copy-done
  36.6 0.5 next_share.1
  37.2 10.6 %all_to_all.22 = f32[16,16,128]{2,1,0:T(8,128)S(1)} all-to-all(f32[16,16,128]{2,1,0:T(8,128)S(1)} %next_share.1), channel_id=1, replica_groups={{0,1,2,3,32,33,34,35,64,65,66,67,96,97,98,99},{4,5,6,7,36,37,38,39,68,6..., dimensions={0} | all-to-all | bytes 262144 | tf_op jit(solution)/shard_map/all_to_all | solution.py:37
  47.9 14.6 %all_to_all.23.sums_ref = f32[32,8,128]{2,1,0:T(8,128)S(1)} all-to-all(f32[32,8,128]{2,1,0:T(8,128)S(1)} %broadcast_in_dim.5), channel_id=1, replica_groups={{280,284,272,276,264,268,256,260,408,412,400,404,392,396,384,388,24,28,..., dimensions={0} | all-to-all | bytes 262144 | tf_op jit(solution)/shard_map/all_to_all | solution.py:37
  62.5 0.7 %last_step.1 = (f32[2,2,2,2,128]{4,3,2,1,0:T(2,128)}, f32[2,2,2,128]{3,2,1,0:T(2,128)}) custom-call(f32[32,8,128]{2,1,0:T(8,128)S(1)} %all_to_all.23.sums_ref, f32[2,2,2,2,128]{4,3,2,1,0:T(2,128)S(1)} %bitcast.11, f32[2,2,2,128]{3,2,1,0:T(2,128)S(1)} %copy-done), custom_call_target="tpu_custom_call" | custom-call | tf_op jit(solution)/shard_map/last_step/pallas_call | solution.py:227
  (13 shorter events, 0.2 us)
Async XLA Ops:
  0.6 36.0 %copy-start = (f32[2,2,2,128]{3,2,1,0:T(2,128)S(1)}, f32[2,2,2,128]{3,2,1,0:T(2,128)}, u32[]{:S(2)}) copy-start(f32[2,2,2,128]{3,2,1,0:T(2,128)} %column_ref) | copy-start | bytes 12292

commit v5 on v4

--- a/solution.py
+++ b/solution.py
@@ -18,8 +18,8 @@
 TA = ("xl", "core")
 NEAR = ("yl", "xh")
 FAR = ("yh", "z")
-NEAR_FIRST = (0, 0)
-FAR_FIRST = (22, 22)
+NEAR_FIRST = (13, 13)
+FAR_FIRST = (21, 21)
 
 
 def second_order(local_green, column):
@@ -247,7 +247,7 @@
     times = lax.axis_size(TA)
     near, far = lax.axis_size(NEAR), lax.axis_size(FAR)
     point_count = points * lax.axis_size(KA)
-    place = lax.axis_index(NEAR)
+    places = [lax.axis_index(NEAR) ^ (first // times) for first in NEAR_FIRST]
     column = impurity_column
     for iteration in range(ITERS):
         first = NEAR_FIRST[iteration] % times
@@ -259,11 +259,11 @@
             share = next_share(
                 self_energy, green_row, factors, own_prev, green_held, hist_held, near, times, first
             )
-        share, place = lax.optimization_barrier((share, place))
+        share, *places = lax.optimization_barrier((share, *places))
         got = spread(share, NEAR + TA, NEAR_FIRST[iteration])
         got, column = lax.optimization_barrier((got, column))
         got = got.reshape(near, times, points, 8, width)
-        own = lax.dynamic_index_in_dim(got, place ^ (NEAR_FIRST[iteration] // times), 0, keepdims=False, allow_negative_indices=False)
+        own = lax.dynamic_index_in_dim(got, places[iteration], 0, keepdims=False, allow_negative_indices=False)
         green_row = jnp.sum(own, axis=0).reshape(points, 2, 2, 2, width)
         near_sum = jnp.sum(got, axis=(0, 1, 2))
         near_sum, green_row = lax.optimization_barrier((near_sum, green_row))

time: 63.4 us -> 61.3 us (0.967)
  blocking collectives: 58.8 us -> 56.2 us
    all_to_all x4, blocking collectives: 58.8 us -> 56.2 us  [spread(): lax.all_to_all(blocks, axes, 0, 0, tiled=True, axis_index_groups=[order])]
where the time goes in v5:
time: 61.3 us; the launch traced here: 60.6 us
  blocking collectives  56.2 us (92%)
  Pallas kernels  3.43 us (6%)
  between operations  0.74 us (1%)
    all_to_all x4, blocking collectives, spread(): lax.all_to_all(blocks, axes, 0, 0, tiled=True, axis_index_groups=[order])  56.2 us
    pallas_call x1, Pallas kernels, first_share(): pl.pallas_call(functools.partial(first_kernel, near, times, first), out_s...  2.23 us

profile of v5, /device:TPU:1, one launch (start us, length us, event | category | flops | bytes accessed | tf_op | source)
XLA Modules:
  0.0 60.6 jit_solution(7451669102001611149)
XLA Ops:
  0.6 0.0 copy-start
  0.6 2.2 %first_share.1 = (f32[16,16,128]{2,1,0:T(8,128)S(1)}, f32[2,4,8,128]{3,2,1,0:T(8,128)S(1)}, f32[16,128]{1,0:T(8,128)S(1)}, bf16[2,4,2,128,512]{4,3,2,1,0:T(8,128)(2,1)S(1)}, bf16[4,2,128,512]{3,2,1,0:T(8,128)(2,1)S(1)}) custom-call(f32[2,2,2,2]{3,2,1,0:T(2,128)} %prop_in.1, f32[2,2,2,128]{3,2,1,0:T(2,128)} %sigma_in.1, f32[2,2,2,2,128]{4,3,2,1,0:T(2,128)} %prev_in.1, ...), custom_call_target="tpu_custom_call" | custom-call | tf_op jit(solution)/shard_map/first_share/pallas_call | solution.py:186
  2.9 14.7 %all_to_all.20 = f32[16,16,128]{2,1,0:T(8,128)S(1)} all-to-all(f32[16,16,128]{2,1,0:T(8,128)S(1)} %get-tuple-element.25), channel_id=1, replica_groups={{97,96,99,98,65,64,67,66,33,32,35,34,1,0,3,2},{101,100,103,102,69,68,71..., dimensions={0} | all-to-all | bytes 262144 | tf_op jit(solution)/shard_map/all_to_all | solution.py:37
  17.6 16.6 %all_to_all.21 = f32[32,8,128]{2,1,0:T(8,128)S(1)} all-to-all(f32[32,8,128]{2,1,0:T(8,128)S(1)} %broadcast_in_dim.4), channel_id=1, replica_groups={{276,272,284,280,260,256,268,264,404,400,412,408,388,384,396,392,20,16,..., dimensions={0} | all-to-all | bytes 262144 | tf_op jit(solution)/shard_map/all_to_all | solution.py:37
  34.3 0.0 copy-done
  34.4 0.5 next_share.1
  34.9 10.1 %all_to_all.22 = f32[16,16,128]{2,1,0:T(8,128)S(1)} all-to-all(f32[16,16,128]{2,1,0:T(8,128)S(1)} %next_share.1), channel_id=1, replica_groups={{97,96,99,98,65,64,67,66,33,32,35,34,1,0,3,2},{101,100,103,102,69,68,71..., dimensions={0} | all-to-all | bytes 262144 | tf_op jit(solution)/shard_map/all_to_all | solution.py:37
  45.1 14.8 %all_to_all.23.sums_ref = f32[32,8,128]{2,1,0:T(8,128)S(1)} all-to-all(f32[32,8,128]{2,1,0:T(8,128)S(1)} %broadcast_in_dim.5), channel_id=1, replica_groups={{276,272,284,280,260,256,268,264,404,400,412,408,388,384,396,392,20,16,..., dimensions={0} | all-to-all | bytes 262144 | tf_op jit(solution)/shard_map/all_to_all | solution.py:37
  59.9 0.7 %last_step.1 = (f32[2,2,2,2,128]{4,3,2,1,0:T(2,128)}, f32[2,2,2,128]{3,2,1,0:T(2,128)}) custom-call(f32[32,8,128]{2,1,0:T(8,128)S(1)} %all_to_all.23.sums_ref, f32[2,2,2,2,128]{4,3,2,1,0:T(2,128)S(1)} %bitcast.11, f32[2,2,2,128]{3,2,1,0:T(2,128)S(1)} %copy-done), custom_call_target="tpu_custom_call" | custom-call | tf_op jit(solution)/shard_map/last_step/pallas_call | solution.py:227
  (13 shorter events, 0.2 us)
Async XLA Ops:
  0.6 33.7 %copy-start = (f32[2,2,2,128]{3,2,1,0:T(2,128)S(1)}, f32[2,2,2,128]{3,2,1,0:T(2,128)}, u32[]{:S(2)}) copy-start(f32[2,2,2,128]{3,2,1,0:T(2,128)} %column_ref) | copy-start | bytes 12292

commit v6 on v5

--- a/solution.py
+++ b/solution.py
@@ -13,13 +13,13 @@
 TIME_STEP = 0.02
 COUPLING = 1.0
 
-CUT = (("yh", 4), ("yl", 2), ("xh", 2), ("z", 8), ("xl", 2), ("core", 2))
-KA = ("yh", "yl", "xh", "z")
+CUT = (("y", 8), ("xh", 2), ("zh", 4), ("zl", 2), ("xl", 2), ("core", 2))
+KA = ("y", "xh", "zh", "zl")
 TA = ("xl", "core")
-NEAR = ("yl", "xh")
-FAR = ("yh", "z")
+NEAR = ("zl", "xh")
+FAR = ("y", "zh")
 NEAR_FIRST = (13, 13)
-FAR_FIRST = (21, 21)
+FAR_FIRST = (18, 18)
 
 
 def second_order(local_green, column):

time: 61.3 us -> 60.6 us (0.989)
  no operation moved by 1% of the time
where the time goes in v6:
time: 60.6 us; the launch traced here: 60.3 us
  blocking collectives  56 us (92%)
  Pallas kernels  3.43 us (6%)
  between operations  0.74 us (1%)
    all_to_all x4, blocking collectives, spread(): lax.all_to_all(blocks, axes, 0, 0, tiled=True, axis_index_groups=[order])  56 us
    pallas_call x1, Pallas kernels, first_share(): pl.pallas_call(functools.partial(first_kernel, near, times, first), out_s...  2.23 us

profile of v6, /device:TPU:1, one launch (start us, length us, event | category | flops | bytes accessed | tf_op | source)
XLA Modules:
  0.0 60.3 jit_solution(5208787808330893063)
XLA Ops:
  0.6 0.0 copy-start
  0.6 2.2 %first_share.1 = (f32[16,16,128]{2,1,0:T(8,128)S(1)}, f32[2,4,8,128]{3,2,1,0:T(8,128)S(1)}, f32[16,128]{1,0:T(8,128)S(1)}, bf16[2,4,2,128,512]{4,3,2,1,0:T(8,128)(2,1)S(1)}, bf16[4,2,128,512]{3,2,1,0:T(8,128)(2,1)S(1)}) custom-call(f32[2,2,2,2]{3,2,1,0:T(2,128)} %prop_in.1, f32[2,2,2,128]{3,2,1,0:T(2,128)} %sigma_in.1, f32[2,2,2,2,128]{4,3,2,1,0:T(2,128)} %prev_in.1, ...), custom_call_target="tpu_custom_call" | custom-call | tf_op jit(solution)/shard_map/first_share/pallas_call | solution.py:186
  2.9 14.7 %all_to_all.20 = f32[16,16,128]{2,1,0:T(8,128)S(1)} all-to-all(f32[16,16,128]{2,1,0:T(8,128)S(1)} %get-tuple-element.25), channel_id=1, replica_groups={{37,36,39,38,5,4,7,6,33,32,35,34,1,0,3,2},{45,44,47,46,13,12,15,14,41,4..., dimensions={0} | all-to-all | bytes 262144 | tf_op jit(solution)/shard_map/all_to_all | solution.py:37
  17.6 16.9 %all_to_all.21 = f32[32,8,128]{2,1,0:T(8,128)S(1)} all-to-all(f32[32,8,128]{2,1,0:T(8,128)S(1)} %broadcast_in_dim.4), channel_id=1, replica_groups={{272,280,256,264,336,344,320,328,400,408,384,392,464,472,448,456,16,24,..., dimensions={0} | all-to-all | bytes 262144 | tf_op jit(solution)/shard_map/all_to_all | solution.py:37
  34.5 0.0 copy-done
  34.6 0.5 next_share.1
  35.1 9.2 %all_to_all.22 = f32[16,16,128]{2,1,0:T(8,128)S(1)} all-to-all(f32[16,16,128]{2,1,0:T(8,128)S(1)} %next_share.1), channel_id=1, replica_groups={{37,36,39,38,5,4,7,6,33,32,35,34,1,0,3,2},{45,44,47,46,13,12,15,14,41,4..., dimensions={0} | all-to-all | bytes 262144 | tf_op jit(solution)/shard_map/all_to_all | solution.py:37
  44.4 15.2 %all_to_all.23.sums_ref = f32[32,8,128]{2,1,0:T(8,128)S(1)} all-to-all(f32[32,8,128]{2,1,0:T(8,128)S(1)} %broadcast_in_dim.5), channel_id=1, replica_groups={{272,280,256,264,336,344,320,328,400,408,384,392,464,472,448,456,16,24,..., dimensions={0} | all-to-all | bytes 262144 | tf_op jit(solution)/shard_map/all_to_all | solution.py:37
  59.7 0.7 %last_step.1 = (f32[2,2,2,2,128]{4,3,2,1,0:T(2,128)}, f32[2,2,2,128]{3,2,1,0:T(2,128)}) custom-call(f32[32,8,128]{2,1,0:T(8,128)S(1)} %all_to_all.23.sums_ref, f32[2,2,2,2,128]{4,3,2,1,0:T(2,128)S(1)} %bitcast.11, f32[2,2,2,128]{3,2,1,0:T(2,128)S(1)} %copy-done), custom_call_target="tpu_custom_call" | custom-call | tf_op jit(solution)/shard_map/last_step/pallas_call | solution.py:227
  (13 shorter events, 0.2 us)
Async XLA Ops:
  0.6 33.9 %copy-start = (f32[2,2,2,128]{3,2,1,0:T(2,128)S(1)}, f32[2,2,2,128]{3,2,1,0:T(2,128)}, u32[]{:S(2)}) copy-start(f32[2,2,2,128]{3,2,1,0:T(2,128)} %column_ref) | copy-start | bytes 12292

commit v7 on v6

--- a/solution.py
+++ b/solution.py
@@ -137,32 +137,37 @@
         propagate_share(near, times, first, k, inner, own_prev[pl.ds(k * 8, 8), :], factors, out_ref)
 
 
-def next_kernel(
-    near, times, first,
-    sigma_ref, row_ref, factor_ref, own_prev, green_ref, hist_ref, out_ref,
-    sigma_lhs, row_lhs,
-):
-    points = row_ref.shape[0]
-    fill_left(sigma_ref, row_ref, sigma_lhs, row_lhs)
-    row_terms = contract(row_lhs, [[hist_ref[j, c] for c in range(2)] for j in range(4)])
-    for k in range(points):
-        inner = contract(sigma_lhs, [[green_ref[k, j, c] for c in range(2)] for j in range(4)])
-        inner = inner + row_terms[k * 8:(k + 1) * 8]
-        factors = [factor_ref[k, j] for j in range(4)]
-        propagate_share(near, times, first, k, inner, own_prev[pl.ds(k * 8, 8), :], factors, out_ref)
-
-
-def last_kernel(
-    point_count, sums_ref, row_ref, column_ref, row_out, energy_out, energy_ref, local_ref, sems,
-):
-    row_copy = pltpu.make_async_copy(row_ref, row_out, sems.at[0])
-    row_copy.start()
+def fill_energy(point_count, sums_ref, column_ref, local_ref, energy_ref):
     local_ref[...] = jnp.sum(sums_ref[...], axis=0) / point_count
     for a in range(2):
         local = [local_ref[pl.ds(o * 4 + a * 2, 2), :] for o in range(2)]
         parts = second_order(local, [column_ref[o, a] for o in range(2)])
         for o in range(2):
             energy_ref[o, a] = parts[o]
+
+
+def next_kernel(
+    near, times, first, point_count,
+    sums_ref, column_ref, row_ref, factor_ref, own_prev, green_ref, hist_ref, out_ref,
+    sigma_lhs, row_lhs, local_ref, sigma_ref,
+):
+    points = row_ref.shape[0]
+    fill_energy(point_count, sums_ref, column_ref, local_ref, sigma_ref)
+    fill_left(sigma_ref, row_ref, sigma_lhs, row_lhs)
+    row_terms = contract(row_lhs, [[hist_ref[j, c] for c in range(2)] for j in range(4)])
+    for k in range(points):
+        inner = contract(sigma_lhs, [[green_ref[k, j, c] for c in range(2)] for j in range(4)])
+        inner = inner + row_terms[k * 8:(k + 1) * 8]
+        factors = [factor_ref[k, j] for j in range(4)]
+        propagate_share(near, times, first, k, inner, own_prev[pl.ds(k * 8, 8), :], factors, out_ref)
+
+
+def last_kernel(
+    point_count, sums_ref, row_ref, column_ref, row_out, energy_out, energy_ref, local_ref, sems,
+):
+    row_copy = pltpu.make_async_copy(row_ref, row_out, sems.at[0])
+    row_copy.start()
+    fill_energy(point_count, sums_ref, column_ref, local_ref, energy_ref)
     energy_copy = pltpu.make_async_copy(energy_ref, energy_out, sems.at[1])
     energy_copy.start()
     row_copy.wait()
@@ -210,17 +215,21 @@
     ))
 
 
-def next_share(self_energy, green_row, factors, own_prev, green_hist, sigma_hist, near, times, first):
+def next_share(sums, column, point_count, green_row, factors, own_prev, green_hist, sigma_hist, near, times, first):
     points, width = green_row.shape[0], green_row.shape[-1]
     return pl.pallas_call(
-        functools.partial(next_kernel, near, times, first),
+        functools.partial(next_kernel, near, times, first, point_count),
         out_shape=jax.ShapeDtypeStruct((near * times, points * 8, width), jnp.float32),
-        in_specs=[VMEM] * 6,
+        in_specs=[VMEM] * 7,
         out_specs=VMEM,
-        scratch_shapes=left_scratch(points, width),
+        scratch_shapes=[
+            *left_scratch(points, width),
+            pltpu.VMEM(sums.shape[1:], jnp.float32),
+            pltpu.VMEM(column.shape, jnp.float32),
+        ],
         compiler_params=pltpu.CompilerParams(vmem_limit_bytes=16 << 20),
         name="next_share",
-    )(self_energy, green_row, factors, own_prev, green_hist, sigma_hist)
+    )(sums, column, green_row, factors, own_prev, green_hist, sigma_hist)
 
 
 def last_step(sums, green_row, column, point_count):
@@ -257,7 +266,7 @@
             )
         else:
             share = next_share(
-                self_energy, green_row, factors, own_prev, green_held, hist_held, near, times, first
+                sums, column, point_count, green_row, factors, own_prev, green_held, hist_held, near, times, first
             )
         share, *places = lax.optimization_barrier((share, *places))
         got = spread(share, NEAR + TA, NEAR_FIRST[iteration])
@@ -269,10 +278,7 @@
         near_sum, green_row = lax.optimization_barrier((near_sum, green_row))
         sums = spread(jnp.broadcast_to(near_sum[None], (far, 8, width)), FAR, FAR_FIRST[iteration])
         sums, green_row = lax.optimization_barrier((sums, green_row))
-        if iteration == ITERS - 1:
-            return last_step(sums, green_row, column, point_count)
-        local_green = (jnp.sum(sums, axis=0) / point_count).reshape(2, 2, 2, width)
-        self_energy = jnp.stack(second_order(local_green, column), axis=0)
+    return last_step(sums, green_row, column, point_count)
 
 
 def solution(mesh):

time: 60.6 us -> 60.5 us (level)
  no operation moved by 1% of the time
where the time goes in v7:
time: 60.5 us; the launch traced here: 60.2 us
  blocking collectives  56 us (93%)
  Pallas kernels  3.43 us (6%)
  between operations  0.72 us (1%)
    all_to_all x4, blocking collectives, spread(): lax.all_to_all(blocks, axes, 0, 0, tiled=True, axis_index_groups=[order])  56 us
    pallas_call x1, Pallas kernels, first_share(): pl.pallas_call(functools.partial(first_kernel, near, times, first), out_s...  2.23 us

profile of v7, /device:TPU:1, one launch (start us, length us, event | category | flops | bytes accessed | tf_op | source)
XLA Modules:
  0.0 60.2 jit_solution(10091771153081549121)
XLA Ops:
  0.6 0.0 copy-start
  0.6 2.2 %first_share.1 = (f32[16,16,128]{2,1,0:T(8,128)S(1)}, f32[2,4,8,128]{3,2,1,0:T(8,128)S(1)}, f32[16,128]{1,0:T(8,128)S(1)}, bf16[2,4,2,128,512]{4,3,2,1,0:T(8,128)(2,1)S(1)}, bf16[4,2,128,512]{3,2,1,0:T(8,128)(2,1)S(1)}) custom-call(f32[2,2,2,2]{3,2,1,0:T(2,128)} %prop_in.1, f32[2,2,2,128]{3,2,1,0:T(2,128)} %sigma_in.1, f32[2,2,2,2,128]{4,3,2,1,0:T(2,128)} %prev_in.1, ...), custom_call_target="tpu_custom_call" | custom-call | tf_op jit(solution)/shard_map/first_share/pallas_call | solution.py:191
  2.9 14.7 %all_to_all.20 = f32[16,16,128]{2,1,0:T(8,128)S(1)} all-to-all(f32[16,16,128]{2,1,0:T(8,128)S(1)} %get-tuple-element.25), channel_id=1, replica_groups={{37,36,39,38,5,4,7,6,33,32,35,34,1,0,3,2},{45,44,47,46,13,12,15,14,41,4..., dimensions={0} | all-to-all | bytes 262144 | tf_op jit(solution)/shard_map/all_to_all | solution.py:37
  17.6 16.9 %all_to_all.21.sums_ref = f32[32,8,128]{2,1,0:T(8,128)S(1)} all-to-all(f32[32,8,128]{2,1,0:T(8,128)S(1)} %broadcast_in_dim.4), channel_id=1, replica_groups={{272,280,256,264,336,344,320,328,400,408,384,392,464,472,448,456,16,24,..., dimensions={0} | all-to-all | bytes 262144 | tf_op jit(solution)/shard_map/all_to_all | solution.py:37
  34.5 0.0 copy-done
  34.5 0.5 next_share.1
  35.0 9.2 %all_to_all.22 = f32[16,16,128]{2,1,0:T(8,128)S(1)} all-to-all(f32[16,16,128]{2,1,0:T(8,128)S(1)} %next_share.1), channel_id=1, replica_groups={{37,36,39,38,5,4,7,6,33,32,35,34,1,0,3,2},{45,44,47,46,13,12,15,14,41,4..., dimensions={0} | all-to-all | bytes 262144 | tf_op jit(solution)/shard_map/all_to_all | solution.py:37
  44.4 15.2 %all_to_all.23.sums_ref = f32[32,8,128]{2,1,0:T(8,128)S(1)} all-to-all(f32[32,8,128]{2,1,0:T(8,128)S(1)} %broadcast_in_dim.5), channel_id=1, replica_groups={{272,280,256,264,336,344,320,328,400,408,384,392,464,472,448,456,16,24,..., dimensions={0} | all-to-all | bytes 262144 | tf_op jit(solution)/shard_map/all_to_all | solution.py:37
  59.6 0.7 %last_step.1 = (f32[2,2,2,2,128]{4,3,2,1,0:T(2,128)}, f32[2,2,2,128]{3,2,1,0:T(2,128)}) custom-call(f32[32,8,128]{2,1,0:T(8,128)S(1)} %all_to_all.23.sums_ref, f32[2,2,2,2,128]{4,3,2,1,0:T(2,128)S(1)} %bitcast.9, f32[2,2,2,128]{3,2,1,0:T(2,128)S(1)} %copy-done), custom_call_target="tpu_custom_call" | custom-call | tf_op jit(solution)/shard_map/last_step/pallas_call | solution.py:236
  (8 shorter events, 0.1 us)
Async XLA Ops:
  0.6 33.9 %copy-start = (f32[2,2,2,128]{3,2,1,0:T(2,128)S(1)}, f32[2,2,2,128]{3,2,1,0:T(2,128)}, u32[]{:S(2)}) copy-start(f32[2,2,2,128]{3,2,1,0:T(2,128)} %column_ref.1) | copy-start | bytes 12292

commit v8 on v7

--- a/solution.py
+++ b/solution.py
@@ -251,12 +251,40 @@
     )(sums, green_row, column)
 
 
+def near_kernel(times, first, got_ref, sum_ref, row_ref):
+    points = row_ref.shape[0]
+    slot = lax.axis_index(NEAR) ^ (first // times)
+    total = jnp.sum(got_ref[...], axis=0)
+    total = sum(total[k * 8:(k + 1) * 8] for k in range(points))
+    sum_ref[...] = jnp.broadcast_to(total[None], sum_ref.shape)
+    own = jnp.sum(got_ref[pl.ds(slot * times, times)], axis=0)
+    for k in range(points):
+        for o in range(2):
+            for a in range(2):
+                at = k * 8 + o * 4 + a * 2
+                row_ref[k, o, a] = own[at:at + 2]
+
+
+def near_step(got, points, times, far, first):
+    width = got.shape[-1]
+    return pl.pallas_call(
+        functools.partial(near_kernel, times, first),
+        out_shape=(
+            jax.ShapeDtypeStruct((far, 8, width), jnp.float32),
+            jax.ShapeDtypeStruct((points, 2, 2, 2, width), jnp.float32),
+        ),
+        in_specs=[VMEM],
+        out_specs=(VMEM,) * 2,
+        compiler_params=pltpu.CompilerParams(vmem_limit_bytes=16 << 20),
+        name="near_step",
+    )(got)
+
+
 def body(green_hist, sigma_hist, prev_row, propagator, impurity_column, sigma_start):
     points, width = prev_row.shape[0], prev_row.shape[-1]
     times = lax.axis_size(TA)
     near, far = lax.axis_size(NEAR), lax.axis_size(FAR)
     point_count = points * lax.axis_size(KA)
-    places = [lax.axis_index(NEAR) ^ (first // times) for first in NEAR_FIRST]
     column = impurity_column
     for iteration in range(ITERS):
         first = NEAR_FIRST[iteration] % times
@@ -268,15 +296,11 @@
             share = next_share(
                 sums, column, point_count, green_row, factors, own_prev, green_held, hist_held, near, times, first
             )
-        share, *places = lax.optimization_barrier((share, *places))
         got = spread(share, NEAR + TA, NEAR_FIRST[iteration])
         got, column = lax.optimization_barrier((got, column))
-        got = got.reshape(near, times, points, 8, width)
-        own = lax.dynamic_index_in_dim(got, places[iteration], 0, keepdims=False, allow_negative_indices=False)
-        green_row = jnp.sum(own, axis=0).reshape(points, 2, 2, 2, width)
-        near_sum = jnp.sum(got, axis=(0, 1, 2))
+        near_sum, green_row = near_step(got, points, times, far, NEAR_FIRST[iteration])
         near_sum, green_row = lax.optimization_barrier((near_sum, green_row))
-        sums = spread(jnp.broadcast_to(near_sum[None], (far, 8, width)), FAR, FAR_FIRST[iteration])
+        sums = spread(near_sum, FAR, FAR_FIRST[iteration])
         sums, green_row = lax.optimization_barrier((sums, green_row))
     return last_step(sums, green_row, column, point_count)
 

time: 60.5 us -> 60.4 us (level)
  no operation moved by 1% of the time
where the time goes in v8:
time: 60.4 us; the launch traced here: 60.1 us
  blocking collectives  56 us (93%)
  Pallas kernels  3.5 us (6%)
  between operations  0.66 us (1%)
    all_to_all x4, blocking collectives, spread(): lax.all_to_all(blocks, axes, 0, 0, tiled=True, axis_index_groups=[order])  56 us
    pallas_call x1, Pallas kernels, first_share(): pl.pallas_call(functools.partial(first_kernel, near, times, first), out_s...  2.24 us

profile of v8, /device:TPU:1, one launch (start us, length us, event | category | flops | bytes accessed | tf_op | source)
XLA Modules:
  0.0 60.1 jit_solution(10934399397720439958)
XLA Ops:
  0.6 0.0 copy-start
  0.6 2.2 %first_share.1 = (f32[16,16,128]{2,1,0:T(8,128)S(1)}, f32[2,4,8,128]{3,2,1,0:T(8,128)S(1)}, f32[16,128]{1,0:T(8,128)S(1)}, bf16[2,4,2,128,512]{4,3,2,1,0:T(8,128)(2,1)S(1)}, bf16[4,2,128,512]{3,2,1,0:T(8,128)(2,1)S(1)}) custom-call(f32[2,2,2,2]{3,2,1,0:T(2,128)} %prop_in.1, f32[2,2,2,128]{3,2,1,0:T(2,128)} %sigma_in.1, f32[2,2,2,2,128]{4,3,2,1,0:T(2,128)} %prev_in.1, ...), custom_call_target="tpu_custom_call" | custom-call | tf_op jit(solution)/shard_map/first_share/pallas_call | solution.py:191
  2.9 14.7 %all_to_all.20.got_ref = f32[16,16,128]{2,1,0:T(8,128)S(1)} all-to-all(f32[16,16,128]{2,1,0:T(8,128)S(1)} %get-tuple-element.19), channel_id=1, replica_groups={{37,36,39,38,5,4,7,6,33,32,35,34,1,0,3,2},{45,44,47,46,13,12,15,14,41,4..., dimensions={0} | all-to-all | bytes 262144 | tf_op jit(solution)/shard_map/all_to_all | solution.py:37
  17.6 16.9 %all_to_all.21.sums_ref = f32[32,8,128]{2,1,0:T(8,128)S(1)} all-to-all(f32[32,8,128]{2,1,0:T(8,128)S(1)} %get-tuple-element.21), channel_id=1, replica_groups={{272,280,256,264,336,344,320,328,400,408,384,392,464,472,448,456,16,24,..., dimensions={0} | all-to-all | bytes 262144 | tf_op jit(solution)/shard_map/all_to_all | solution.py:37
  34.4 0.0 copy-done
  34.4 0.6 next_share.1
  35.0 9.2 %all_to_all.22.got_ref = f32[16,16,128]{2,1,0:T(8,128)S(1)} all-to-all(f32[16,16,128]{2,1,0:T(8,128)S(1)} %next_share.1), channel_id=1, replica_groups={{37,36,39,38,5,4,7,6,33,32,35,34,1,0,3,2},{45,44,47,46,13,12,15,14,41,4..., dimensions={0} | all-to-all | bytes 262144 | tf_op jit(solution)/shard_map/all_to_all | solution.py:37
  44.3 15.2 %all_to_all.23.sums_ref = f32[32,8,128]{2,1,0:T(8,128)S(1)} all-to-all(f32[32,8,128]{2,1,0:T(8,128)S(1)} %get-tuple-element.31), channel_id=1, replica_groups={{272,280,256,264,336,344,320,328,400,408,384,392,464,472,448,456,16,24,..., dimensions={0} | all-to-all | bytes 262144 | tf_op jit(solution)/shard_map/all_to_all | solution.py:37
  59.5 0.7 %last_step.1 = (f32[2,2,2,2,128]{4,3,2,1,0:T(2,128)}, f32[2,2,2,128]{3,2,1,0:T(2,128)}) custom-call(f32[32,8,128]{2,1,0:T(8,128)S(1)} %all_to_all.23.sums_ref, f32[2,2,2,2,128]{4,3,2,1,0:T(2,128)S(1)} %get-tuple-element.34.row_ref, f32[2,2,2,128]{3,2,1,0:T(2,128)S(1)} %copy-done), custom_call_target="tpu_custom_call" | custom-call | tf_op jit(solution)/shard_map/last_step/pallas_call | solution.py:236
  (2 shorter events, 0.1 us)
Async XLA Ops:
  0.6 33.8 %copy-start = (f32[2,2,2,128]{3,2,1,0:T(2,128)S(1)}, f32[2,2,2,128]{3,2,1,0:T(2,128)}, u32[]{:S(2)}) copy-start(f32[2,2,2,128]{3,2,1,0:T(2,128)} %column_ref.1) | copy-start | bytes 12292

commit v9 on v7

--- a/solution.py
+++ b/solution.py
@@ -19,7 +19,7 @@
 NEAR = ("zl", "xh")
 FAR = ("y", "zh")
 NEAR_FIRST = (13, 13)
-FAR_FIRST = (18, 18)
+FAR_FIRST = (19, 18)
 
 
 def second_order(local_green, column):

time: 60.5 us -> 61.2 us (1.012)
  blocking collectives: 56 us -> 56.7 us
    all_to_all x4, blocking collectives: 56 us -> 56.7 us  [spread(): lax.all_to_all(blocks, axes, 0, 0, tiled=True, axis_index_groups=[order])]
where the time goes in v9:
time: 61.2 us; the launch traced here: 61 us
  blocking collectives  56.7 us (93%)
  Pallas kernels  3.43 us (6%)
  between operations  0.72 us (1%)
    all_to_all x4, blocking collectives, spread(): lax.all_to_all(blocks, axes, 0, 0, tiled=True, axis_index_groups=[order])  56.7 us
    pallas_call x1, Pallas kernels, first_share(): pl.pallas_call(functools.partial(first_kernel, near, times, first), out_s...  2.23 us

profile of v9, /device:TPU:1, one launch (start us, length us, event | category | flops | bytes accessed | tf_op | source)
XLA Modules:
  0.0 61.0 jit_solution(3999441771472548333)
XLA Ops:
  0.6 0.0 copy-start
  0.6 2.2 %first_share.1 = (f32[16,16,128]{2,1,0:T(8,128)S(1)}, f32[2,4,8,128]{3,2,1,0:T(8,128)S(1)}, f32[16,128]{1,0:T(8,128)S(1)}, bf16[2,4,2,128,512]{4,3,2,1,0:T(8,128)(2,1)S(1)}, bf16[4,2,128,512]{3,2,1,0:T(8,128)(2,1)S(1)}) custom-call(f32[2,2,2,2]{3,2,1,0:T(2,128)} %prop_in.1, f32[2,2,2,128]{3,2,1,0:T(2,128)} %sigma_in.1, f32[2,2,2,2,128]{4,3,2,1,0:T(2,128)} %prev_in.1, ...), custom_call_target="tpu_custom_call" | custom-call | tf_op jit(solution)/shard_map/first_share/pallas_call | solution.py:191
  2.9 14.7 %all_to_all.20 = f32[16,16,128]{2,1,0:T(8,128)S(1)} all-to-all(f32[16,16,128]{2,1,0:T(8,128)S(1)} %get-tuple-element.25), channel_id=1, replica_groups={{37,36,39,38,5,4,7,6,33,32,35,34,1,0,3,2},{45,44,47,46,13,12,15,14,41,4..., dimensions={0} | all-to-all | bytes 262144 | tf_op jit(solution)/shard_map/all_to_all | solution.py:37
  17.6 17.5 %all_to_all.21.sums_ref = f32[32,8,128]{2,1,0:T(8,128)S(1)} all-to-all(f32[32,8,128]{2,1,0:T(8,128)S(1)} %broadcast_in_dim.4), channel_id=1, replica_groups={{280,272,264,256,344,336,328,320,408,400,392,384,472,464,456,448,24,16,..., dimensions={0} | all-to-all | bytes 262144 | tf_op jit(solution)/shard_map/all_to_all | solution.py:37
  35.1 0.0 copy-done
  35.1 0.5 next_share.1
  35.7 9.3 %all_to_all.22 = f32[16,16,128]{2,1,0:T(8,128)S(1)} all-to-all(f32[16,16,128]{2,1,0:T(8,128)S(1)} %next_share.1), channel_id=1, replica_groups={{37,36,39,38,5,4,7,6,33,32,35,34,1,0,3,2},{45,44,47,46,13,12,15,14,41,4..., dimensions={0} | all-to-all | bytes 262144 | tf_op jit(solution)/shard_map/all_to_all | solution.py:37
  45.0 15.3 %all_to_all.23.sums_ref = f32[32,8,128]{2,1,0:T(8,128)S(1)} all-to-all(f32[32,8,128]{2,1,0:T(8,128)S(1)} %broadcast_in_dim.5), channel_id=1, replica_groups={{272,280,256,264,336,344,320,328,400,408,384,392,464,472,448,456,16,24,..., dimensions={0} | all-to-all | bytes 262144 | tf_op jit(solution)/shard_map/all_to_all | solution.py:37
  60.3 0.7 %last_step.1 = (f32[2,2,2,2,128]{4,3,2,1,0:T(2,128)}, f32[2,2,2,128]{3,2,1,0:T(2,128)}) custom-call(f32[32,8,128]{2,1,0:T(8,128)S(1)} %all_to_all.23.sums_ref, f32[2,2,2,2,128]{4,3,2,1,0:T(2,128)S(1)} %bitcast.9, f32[2,2,2,128]{3,2,1,0:T(2,128)S(1)} %copy-done), custom_call_target="tpu_custom_call" | custom-call | tf_op jit(solution)/shard_map/last_step/pallas_call | solution.py:236
  (8 shorter events, 0.1 us)
Async XLA Ops:
  0.6 34.5 %copy-start = (f32[2,2,2,128]{3,2,1,0:T(2,128)S(1)}, f32[2,2,2,128]{3,2,1,0:T(2,128)}, u32[]{:S(2)}) copy-start(f32[2,2,2,128]{3,2,1,0:T(2,128)} %column_ref.1) | copy-start | bytes 12292
